TPU v7x, 32 devices: a whole 2x2x4 slice. The times are simulated.
32 devices in a mesh: groups: 2 (over y), wide: 8 (over z, x), narrow: 2 (over core).
Axes of the slice: x: 2, y: 2, z: 4, core: 2. Of those that a mesh axis runs over, the one named last changes fastest.
Arguments:
- goals: float32 [8192, 1024], P(('groups', 'wide', 'narrow')), parts along dimension 0, may hold values from -32 to 32
- premises: float32 [1024, 1024], P(('groups', 'wide', 'narrow')), parts along dimension 0, may hold values from -24 to 24
- counts: int32 [8192], P(('groups', 'wide')), parts along dimension 0, may hold values from 1 to 16
- positives: int32 [8192, 16], P(('groups', 'wide')), parts along dimension 0, may hold values from -1 to 511, as said below
- cotangent: float32 [8192], P(('groups', 'wide')), parts along dimension 0, may hold values from -6 to 6
Outputs:
- goal_loss: float32 [8192], P(('groups', 'wide')), parts along dimension 0
- grad_goals: float32 [8192, 1024], P(('groups', 'wide', 'narrow')), parts along dimension 0
- grad_premises: float32 [1024, 1024], P(('groups', 'wide', 'narrow')), parts along dimension 0
There are 2 independent parts, one for each index of `groups`. A program takes and returns all parts, laid end to end along the dimension named above; each array names one. Nothing has to cross between parts.
Inputs may be any that keep to these rules, and one draw needn't show every extreme that they name: positives[i, k] is a premise index for k < counts[i] and -1 from there on.
All inputs are finite; a program needn't handle non-finite values.
Results may differ from a plain program's by a relative error of at most 0.012.
The roundings to bfloat16 on the way count: a program that leaves them out, or rounds other values in their place, can miss the bound.
Values may be sent and summed in bfloat16 or wider, within the bound.
A program may use at most 64 MiB of HBM per device.

v0:
```python
import jax
import jax.numpy as jnp
from jax import lax
from jax.sharding import PartitionSpec as P


def hit_counts(row_lists, column_ids):
    total = jnp.zeros((row_lists.shape[0], column_ids.shape[0]), jnp.float32)
    for which_slot in range(row_lists.shape[1]):
        total = total + (row_lists[:, which_slot][:, None] == column_ids[None, :]).astype(
            jnp.float32
        )
    return total


def per_device(goals, premises, counts, positives, cotangent):
    goal_part = goals.astype(jnp.bfloat16)
    prem_part = premises.astype(jnp.bfloat16)
    prem_rows = prem_part.shape[0]
    width = goal_part.shape[1]
    scale = width ** (-0.5)
    n_wide = lax.axis_size("wide")
    n_narrow = lax.axis_size("narrow")
    narrow_index = lax.axis_index("narrow")
    rows_block = lax.all_gather(goal_part, "narrow", axis=0, tiled=True)
    prem_block = lax.all_gather(prem_part, "wide", axis=0, tiled=True)
    goal_counts = counts.astype(jnp.float32)
    local_ids = jnp.arange(prem_rows * n_wide, dtype=jnp.int32)
    column_ids = (
        local_ids // prem_rows * n_narrow + narrow_index
    ) * prem_rows + local_ids % prem_rows
    col_total = prem_block.shape[0]
    row_total = rows_block.shape[0]
    step_cols = 512 if col_total % 512 == 0 else col_total
    starts = list(range(0, col_total, step_cols))

    def tile_scores(begin):
        piece = prem_block[begin : begin + step_cols]
        return (
            lax.dot_general(
                rows_block, piece, (((1,), (1,)), ((), ())), preferred_element_type=jnp.float32
            )
            * scale
        )

    top = jnp.full((row_total,), -jnp.inf, jnp.float32)
    total = jnp.zeros((row_total,), jnp.float32)
    positive_sum = jnp.zeros((row_total,), jnp.float32)
    for begin in starts:
        scores = tile_scores(begin)
        hits = hit_counts(positives, column_ids[begin : begin + step_cols])
        new_top = jnp.maximum(top, jnp.max(scores, axis=1))
        total = total * jnp.exp(top - new_top) + jnp.sum(jnp.exp(scores - new_top[:, None]), axis=1)
        positive_sum = positive_sum + jnp.sum(hits * scores, axis=1)
        top = new_top
    best = lax.pmax(top, "narrow")
    total_all, positive_all = lax.psum((total * jnp.exp(top - best), positive_sum), "narrow")
    log_total = best + jnp.log(total_all)
    row_loss = log_total - positive_all / goal_counts
    grad_rows = jnp.zeros((row_total, width), jnp.float32)
    pieces = []
    for number, begin in enumerate(starts):
        scores = tile_scores(begin)
        hits = hit_counts(positives, column_ids[begin : begin + step_cols])
        dscores = (
            cotangent[:, None]
            * (jnp.exp(scores - log_total[:, None]) - hits / goal_counts[:, None])
            * scale
        ).astype(jnp.bfloat16)
        grad_rows = grad_rows + jnp.dot(
            dscores, prem_block[begin : begin + step_cols], preferred_element_type=jnp.float32
        )
        pieces.append(dscores)
    stored = jnp.concatenate(pieces, axis=1)
    grad_goals = lax.psum_scatter(grad_rows, "narrow", scatter_dimension=0, tiled=True)
    grad_premises = lax.psum_scatter(
        lax.dot_general(
            stored, rows_block, (((0,), (0,)), ((), ())), preferred_element_type=jnp.float32
        ),
        "wide",
        scatter_dimension=0,
        tiled=True,
    )
    return (row_loss, grad_goals, grad_premises)


def solution(mesh):
    return jax.shard_map(
        per_device,
        mesh=mesh,
        in_specs=(
            P(("groups", "wide", "narrow"), None),
            P(("groups", "wide", "narrow"), None),
            P(("groups", "wide")),
            P(("groups", "wide"), None),
            P(("groups", "wide")),
        ),
        out_specs=(
            P(("groups", "wide")),
            P(("groups", "wide", "narrow"), None),
            P(("groups", "wide", "narrow"), None),
        ),
        check_vma=False,
    )
```

profile of v0, /device:TPU:0, one launch (start us, length us, event | category | flops | bytes accessed | tf_op | source)
XLA Modules:
  0.0 136.1 jit_solution(13301415830657365863)
XLA Ops:
  7.2 0.0 copy-start.2
  7.2 0.0 copy-start
  7.2 0.0 copy-start.1
  7.2 0.0 all-gather.2.cloned.1.call-start
  7.2 2.1 %convert_element_type.76 = bf16[256,1024]{1,0:T(8,128)(2,1)} convert(f32[256,1024]{1,0:T(8,128)} %param.5) | non-fusion elementwise | flops 262144 | bytes 1572864 | tf_op jit(solution)/shard_map/convert_element_type | solution.py:17
  9.4 0.0 copy-start.4
  9.4 0.0 all-gather.2.cloned.1.call-update
  9.4 0.0 reduce-scatter.5.cloned.1.call-start
  9.4 0.0 copy-done.2
  9.5 0.0 copy-done
  9.5 0.0 copy-done.1
  9.6 33.0 %all_gather.7 = bf16[256,1024]{1,0:T(8,128)(2,1)S(1)} all-gather(bf16[32,1024]{1,0:T(8,128)(2,1)S(1)} %convert_element_type.77), channel_id=1, replica_groups=mesh['groups'=2,'wide'=8,'narrow'=2] {'wide'}, dimensions={0}, use_global_device_ids=true | all-gather | bytes 589824 | tf_op jit(solution)/shard_map/all_gather | solution.py:26
  42.6 0.0 all-gather.2.cloned.1.call-done
  42.6 0.0 copy-start.3
  42.6 1.8 %fusion.9 = (f32[512]{0:T(512)S(1)}, f32[512,256]{0,1:T(8,128)S(1)}) fusion(bf16[512,1024]{1,0:T(8,128)(2,1)} %all-gather.2.cloned.1.call-done, bf16[256,1024]{1,0:T(8,128)(2,1)S(1)} %all_gather.7), kind=kOutput, calls=%fused_computation.22 | convolution fusion | flops 268697088 | bytes 2099200 | tf_op jit(solution)/shard_map/dot_general | solution.py:40
  44.4 2.5 %pmax.7 = f32[512]{0:T(512)S(1)} all-reduce(f32[512]{0:T(512)S(1)} %get-tuple-element.25), channel_id=1, replica_groups=mesh['groups'=2,'wide'=8,'narrow'=2] {'narrow'}, use_global_device_ids=true, to_apply=%region_1.2 | all-reduce | flops 512 | bytes 4096 | tf_op jit(solution)/shard_map/pmax | solution.py:56
  46.9 1.1 multiply_reduce_fusion
  47.9 2.5 %all-reduce = (f32[512]{0:T(512)S(1)}, f32[512]{0:T(512)S(1)}) all-reduce(f32[512]{0:T(512)S(1)} %exponential_multiply_fusion, f32[512]{0:T(512)S(1)} %get-tuple-element.3), channel_id=1, replica_groups=mesh['groups'=2,'wide'=8,'narrow'=2] {'narrow'}, use_global_device_ids=true, to_apply=%region_3.4 | all-reduce | flops 1024 | bytes 8192 | tf_op jit(solution)/shard_map/psum | solution.py:57
  50.4 0.6 divide_subtract_fusion
  51.0 0.0 copy-done.4
  51.0 0.0 copy-done.3
  51.0 2.3 %fusion.6 = f32[256,1024]{1,0:T(8,128)} fusion(bf16[512,1024]{1,0:T(8,128)(2,1)S(1)} %copy-done.3, f32[512,256]{0,1:T(8,128)S(1)} %get-tuple-element.26, f32[512]{0:T(512)S(1)} %convert_element_type.94, f32[512]{0:T(512)S(1)} %get-tuple-element.8, f32[512]{0:T(512)S(1)} %copy-done.4, s32[512]{0:T(512)S(1)} %bitcast.63, s32[512]{0:T(512)S(1)} %bitcast.66, ...), kind=kOutput, calls=%fused_computation.19 | convolution fusion | flops 275382272 | bytes 2661376 | tf_op jit(solution)/shard_map/dot_general | solution.py:77
  53.3 0.0 reduce-scatter.5.cloned.1.call-update
  53.3 0.0 reduce-scatter.3.cloned.1.call-start
  53.4 2.7 %fusion.7 = f32[512,1024]{1,0:T(8,128)} fusion(bf16[256,1024]{1,0:T(8,128)(2,1)S(1)} %all_gather.7, f32[512,256]{0,1:T(8,128)S(1)} %get-tuple-element.26, f32[512]{0:T(512)S(1)} %convert_element_type.94, f32[512]{0:T(512)S(1)} %get-tuple-element.8, f32[512]{0:T(512)S(1)} %copy-done.4, s32[512]{0:T(512)S(1)} %bitcast.64, s32[512]{0:T(512)S(1)} %bitcast.67, ...), kind=kOutput, calls=%fused_computation.20 | convolution fusion | flops 275382272 | bytes 3185664 | tf_op jit(solution)/shard_map/dot_general | solution.py:70
  56.1 0.0 reduce-scatter.3.cloned.1.call-update
  56.1 61.9 %reduce-scatter.5.cloned.1.call-done = f32[32,1024]{1,0:T(8,128)} async-done(((f32[256,1024]{1,0:T(8,128)}), f32[32,1024]{1,0:T(8,128)}) %reduce-scatter.5.cloned.1.call-update) | async-done | bytes 131088 | tf_op jit(solution)/shard_map/reduce_scatter | solution.py:76
  118.0 11.6 %reduce-scatter.3.cloned.1.call-done = f32[256,1024]{1,0:T(8,128)} async-done(((f32[512,1024]{1,0:T(8,128)}), f32[256,1024]{1,0:T(8,128)}) %reduce-scatter.3.cloned.1.call-update) | async-done | bytes 1048592 | tf_op jit(solution)/shard_map/reduce_scatter | solution.py:75
  (5 shorter events, 0.1 us)
Async XLA Ops:
  7.2 2.3 %copy-start.2 = (s32[512]{0:T(512)S(1)}, s32[512]{0:T(512)}, u32[]{:S(2)}) copy-start(s32[512]{0:T(512)} %param.7) | copy-start | bytes 6148
  7.2 2.3 %copy-start = (f32[32,1024]{1,0:T(8,128)S(1)}, f32[32,1024]{1,0:T(8,128)}, u32[]{:S(2)}) copy-start(f32[32,1024]{1,0:T(8,128)} %param.6) | copy-start | bytes 393220
  7.2 2.3 %copy-start.1 = (s32[512,16]{0,1:T(8,128)S(1)}, s32[512,16]{0,1:T(8,128)}, u32[]{:S(2)}) copy-start(s32[512,16]{0,1:T(8,128)} %param.8) | copy-start | bytes 98308
  7.2 35.4 %all-gather.2.cloned.1.call-start = ((), (), s32[]{:S(2)}) async-start(), calls=%async_computation.2 | async-start | bytes 1572864 | tf_op jit(solution)/shard_map/all_gather | solution.py:25
  9.4 41.6 %copy-start.4 = (f32[512]{0:T(512)S(1)}, f32[512]{0:T(512)}, u32[]{:S(2)}) copy-start(f32[512]{0:T(512)} %param.9) | copy-start | bytes 6148
  9.4 108.6 %reduce-scatter.5.cloned.1.call-start = ((), (), s32[]{:S(2)}) async-start(), calls=%async_computation.4 | async-start | bytes 1179648 | tf_op jit(solution)/shard_map/reduce_scatter | solution.py:76
  42.6 8.4 %copy-start.3 = (bf16[512,1024]{1,0:T(8,128)(2,1)S(1)}, bf16[512,1024]{1,0:T(8,128)(2,1)}, u32[]{:S(2)}) copy-start(bf16[512,1024]{1,0:T(8,128)(2,1)} %all-gather.2.cloned.1.call-done) | copy-start | bytes 3145732
  53.3 76.3 %reduce-scatter.3.cloned.1.call-start = ((), (), s32[]{:S(2)}) async-start(), calls=%async_computation.3 | async-start | bytes 3145728 | tf_op jit(solution)/shard_map/reduce_scatter | solution.py:75
Sparse Core Ops, SparseCore 0:
  10.1 11.7 all-gather.1
  53.4 64.5 reduce-scatter.4
  120.9 8.6 reduce-scatter.2
where the time goes:
time: 136 us
  waiting for transfers between devices  73.5 us (54%)
  blocking collectives  38 us (28%)
  between operations  13.8 us (10%)
  matrix products  6.82 us (5%)
  other arithmetic  3.82 us (3%)
    reduce_scatter x1, waiting for transfers between devices, per_device(): lax.psum_scatter(lax.dot_general(stored, rows_block, (((0,), (0,)), ((),...  61.9 us
    all_gather x1, blocking collectives, per_device(): prem_block = lax.all_gather(prem_part, 'wide', axis=0, tiled=True)  33 us
    reduce_scatter x1, waiting for transfers between devices, per_device(): lax.psum_scatter(grad_rows, 'narrow', scatter_dimension=0, tiled=True)  11.6 us
    dot_general x1, matrix products, per_device(): jnp.dot(dscores, prem_block[begin:begin + step_cols], preferred_element_t...  2.73 us
  transfers between devices with their start and end apart: 3, of which 2 were waited for; matrix products, arithmetic and copies ran while one was open for 2% of the time, Pallas kernels for 0%

commit v1 on v0

--- a/solution.py
+++ b/solution.py
@@ -2,6 +2,7 @@
 import jax.numpy as jnp
 from jax import lax
 from jax.sharding import PartitionSpec as P
+from jax.lax import axis_index, ppermute, psum
 
 
 def hit_counts(row_lists, column_ids):
@@ -23,7 +24,29 @@
     n_narrow = lax.axis_size("narrow")
     narrow_index = lax.axis_index("narrow")
     rows_block = lax.all_gather(goal_part, "narrow", axis=0, tiled=True)
-    prem_block = lax.all_gather(prem_part, "wide", axis=0, tiled=True)
+    block_last = psum(1, "wide")
+    local_part = axis_index("wide")
+    piece_next, all_values, raw_out = (block_last, local_part, prem_part.shape[0])
+    runs = [(hop_no, (hop_no + 1) % piece_next) for hop_no in range(piece_next)]
+    heap = [(hop_no, (hop_no - 1) % piece_next) for hop_no in range(piece_next)]
+    prem_block = jnp.zeros(
+        (*prem_part.shape[:0], piece_next * raw_out, *prem_part.shape[1:]), prem_part.dtype
+    )
+    prem_block = lax.dynamic_update_slice_in_dim(
+        prem_block, prem_part, all_values * raw_out, axis=0
+    )
+    s_next = work_now = prem_part
+    everything = piece_next // 2
+    for tick in tuple(range(1, everything + 1)):
+        s_next = ppermute(s_next, "wide", perm=runs)
+        prem_block = lax.dynamic_update_slice_in_dim(
+            prem_block, s_next, (all_values - tick) % piece_next * raw_out, axis=0
+        )
+        if tick < piece_next - everything:
+            work_now = ppermute(work_now, "wide", heap)
+            prem_block = lax.dynamic_update_slice_in_dim(
+                prem_block, work_now, (all_values + tick) % piece_next * raw_out, axis=0
+            )
     goal_counts = counts.astype(jnp.float32)
     local_ids = jnp.arange(prem_rows * n_wide, dtype=jnp.int32)
     column_ids = (

time: 136 us -> 128 us (0.941)
  blocking collectives: 38 us -> 4.94 us
  starting transfers between devices: 0.12 us -> 15.6 us
  waiting for transfers between devices: 73.5 us -> 81.3 us
    all_gather x1 -> x0, blocking collectives: 33 us -> none  [per_device(): prem_block = lax.all_gather(prem_part, 'wide', axis=0, tiled=True)]
    ppermute x0 -> x7, starting transfers between devices: none -> 15.5 us  [the longest x3 12.5 us: per_device(): work_now = ppermute(work_now, 'wide', heap)]
    ppermute x0 -> x7, waiting for transfers between devices: none -> 11.4 us  [the longest x4 11.3 us: per_device(): s_next = ppermute(s_next, 'wide', perm=runs)]
    reduce_scatter x1, waiting for transfers between devices: 61.9 us -> 58.2 us  [per_device(): lax.psum_scatter(lax.dot_general(stored, rows_block, (((0,), (0,)), ((),...]
  transfers between devices with their start and end apart: 3 -> 10, of which waited for: 2 -> 6; matrix products, arithmetic and copies ran while one was open for 2% -> 4% of each run, Pallas kernels for 0% -> 0%
where the time goes in v1:
time: 128 us
  waiting for transfers between devices  81.3 us (64%)
  starting transfers between devices  15.6 us (12%)
  between operations  14.1 us (11%)
  matrix products  6.8 us (5%)
  blocking collectives  4.94 us (4%)
  other arithmetic  4.71 us (4%)
    reduce_scatter x1, waiting for transfers between devices, per_device(): lax.psum_scatter(lax.dot_general(stored, rows_block, (((0,), (0,)), ((),...  58.2 us
    ppermute x3, starting transfers between devices, per_device(): work_now = ppermute(work_now, 'wide', heap)  12.5 us
    reduce_scatter x1, waiting for transfers between devices, per_device(): lax.psum_scatter(grad_rows, 'narrow', scatter_dimension=0, tiled=True)  11.6 us
    ppermute x4, waiting for transfers between devices, per_device(): s_next = ppermute(s_next, 'wide', perm=runs)  11.3 us
    ppermute x4, starting transfers between devices, per_device(): s_next = ppermute(s_next, 'wide', perm=runs)  3.05 us
    dot_general x1, matrix products, per_device(): jnp.dot(dscores, prem_block[begin:begin + step_cols], preferred_element_t...  2.72 us
  transfers between devices with their start and end apart: 10, of which 6 were waited for; matrix products, arithmetic and copies ran while one was open for 4% of the time, Pallas kernels for 0%

profile of v1, /device:TPU:0, one launch (start us, length us, event | category | flops | bytes accessed | tf_op | source)
XLA Modules:
  0.0 127.6 jit_solution(5284921674256027413)
XLA Ops:
  7.2 0.0 copy-start.2
  7.2 0.0 copy-start.1
  7.2 0.0 all-gather.2.cloned.1.call-start
  7.2 0.1 broadcast_in_dim.6
  7.3 0.9 constant_dynamic-update-slice_fusion.7
  8.2 3.0 %collective-permute-start = (bf16[32,1024]{1,0:T(8,128)(2,1)S(1)}, bf16[32,1024]{1,0:T(8,128)(2,1)S(1)}, u32[]{:S(2)}, u32[]{:S(2)}) collective-permute-start(bf16[32,1024]{1,0:T(8,128)(2,1)S(1)} %get-tuple-element.10), channel_id=1, source_target_pairs={{0,2},{2,4},{4,6},{6,8},{8,10},{10,12},{12,14},{14,0},{1,3},{3,5},... | collective-permute-start | bytes 196616 | tf_op jit(solution)/shard_map/ppermute | solution.py:41
  11.2 3.1 %collective-permute-start.1 = (bf16[32,1024]{1,0:T(8,128)(2,1)S(1)}, bf16[32,1024]{1,0:T(8,128)(2,1)S(1)}, u32[]{:S(2)}, u32[]{:S(2)}) collective-permute-start(bf16[32,1024]{1,0:T(8,128)(2,1)S(1)} %get-tuple-element.10), channel_id=1, source_target_pairs={{0,14},{2,0},{4,2},{6,4},{8,6},{10,8},{12,10},{14,12},{1,15},{3,1}... | collective-permute-start | bytes 196616 | tf_op jit(solution)/shard_map/ppermute | solution.py:46
  14.3 2.1 %convert_element_type.77 = bf16[256,1024]{1,0:T(8,128)(2,1)} convert(f32[256,1024]{1,0:T(8,128)} %param.5) | non-fusion elementwise | flops 262144 | bytes 1572864 | tf_op jit(solution)/shard_map/convert_element_type | solution.py:18
  16.4 0.0 all-gather.2.cloned.1.call-update
  16.4 0.0 copy-start.3
  16.4 0.0 reduce-scatter.5.cloned.1.call-start
  16.6 0.0 copy-done.2
  16.7 0.0 copy-done.1
  16.7 0.0 collective-permute-done
  16.8 0.1 collective-permute-start.2
  16.8 0.1 collective-permute-done.1
  16.9 4.6 %collective-permute-start.3 = (bf16[32,1024]{1,0:T(8,128)(2,1)S(1)}, bf16[32,1024]{1,0:T(8,128)(2,1)S(1)}, u32[]{:S(2)}, u32[]{:S(2)}) collective-permute-start(bf16[32,1024]{1,0:T(8,128)(2,1)S(1)} %collective-permute-done.1), channel_id=1, source_target_pairs={{0,14},{2,0},{4,2},{6,4},{8,6},{10,8},{12,10},{14,12},{1,15},{3,1}... | collective-permute-start | bytes 196616 | tf_op jit(solution)/shard_map/ppermute | solution.py:46
  21.6 2.2 %collective-permute-done.2 = bf16[32,1024]{1,0:T(8,128)(2,1)S(1)} collective-permute-done((bf16[32,1024]{1,0:T(8,128)(2,1)S(1)}, bf16[32,1024]{1,0:T(8,128)(2,1)S(1)}, u32[]{:S(2)}, u32[]{:S(2)}) %collective-permute-start.2) | collective-permute-done | bytes 65568 | tf_op jit(solution)/shard_map/ppermute | solution.py:41
  23.8 0.0 collective-permute-start.4
  23.8 0.0 collective-permute-done.3
  23.8 4.7 %collective-permute-start.5 = (bf16[32,1024]{1,0:T(8,128)(2,1)S(1)}, bf16[32,1024]{1,0:T(8,128)(2,1)S(1)}, u32[]{:S(2)}, u32[]{:S(2)}) collective-permute-start(bf16[32,1024]{1,0:T(8,128)(2,1)S(1)} %collective-permute-done.3), channel_id=1, source_target_pairs={{0,14},{2,0},{4,2},{6,4},{8,6},{10,8},{12,10},{14,12},{1,15},{3,1}... | collective-permute-start | bytes 196616 | tf_op jit(solution)/shard_map/ppermute | solution.py:46
  28.5 2.2 %collective-permute-done.4 = bf16[32,1024]{1,0:T(8,128)(2,1)S(1)} collective-permute-done((bf16[32,1024]{1,0:T(8,128)(2,1)S(1)}, bf16[32,1024]{1,0:T(8,128)(2,1)S(1)}, u32[]{:S(2)}, u32[]{:S(2)}) %collective-permute-start.4) | collective-permute-done | bytes 65568 | tf_op jit(solution)/shard_map/ppermute | solution.py:41
  30.7 0.0 collective-permute-start.6
  30.7 0.0 collective-permute-done.5
  30.8 6.9 %collective-permute-done.6 = bf16[32,1024]{1,0:T(8,128)(2,1)S(1)} collective-permute-done((bf16[32,1024]{1,0:T(8,128)(2,1)S(1)}, bf16[32,1024]{1,0:T(8,128)(2,1)S(1)}, u32[]{:S(2)}, u32[]{:S(2)}) %collective-permute-start.6) | collective-permute-done | bytes 65568 | tf_op jit(solution)/shard_map/ppermute | solution.py:41
  37.7 0.0 all-gather.2.cloned.1.call-done
  37.7 0.0 copy-start
  37.7 1.8 %fusion.19 = (f32[512]{0:T(512)S(1)}, f32[256,512]{1,0:T(8,128)S(1)}) fusion(bf16[256,1024]{1,0:T(8,128)(2,1)S(1)} %constant_dynamic-update-slice_fusion, bf16[512,1024]{1,0:T(8,128)(2,1)} %all-gather.2.cloned.1.call-done), kind=kOutput, calls=%fused_computation.38 | convolution fusion | flops 268697088 | bytes 2099200 | tf_op jit(solution)/shard_map/dot_general | solution.py:63
  39.6 2.5 %pmax.7 = f32[512]{0:T(512)S(1)} all-reduce(f32[512]{0:T(512)S(1)} %get-tuple-element.27), channel_id=1, replica_groups=mesh['groups'=2,'wide'=8,'narrow'=2] {'narrow'}, use_global_device_ids=true, to_apply=%region_1.2 | all-reduce | flops 512 | bytes 4096 | tf_op jit(solution)/shard_map/pmax | solution.py:79
  42.0 1.1 fusion.2
  43.1 2.5 %all-reduce = (f32[512]{0:T(512)S(1)}, f32[512]{0:T(512)S(1)}) all-reduce(f32[512]{0:T(512)S(1)} %exponential_multiply_fusion, f32[512]{0:T(512)S(1)} %get-tuple-element.3), channel_id=1, replica_groups=mesh['groups'=2,'wide'=8,'narrow'=2] {'narrow'}, use_global_device_ids=true, to_apply=%region_3.4 | all-reduce | flops 1024 | bytes 8192 | tf_op jit(solution)/shard_map/psum | solution.py:80
  45.6 0.6 divide_subtract_fusion
  46.2 0.0 copy-done.3
  46.2 0.0 copy-done
  46.2 2.3 %fusion.14 = f32[256,1024]{1,0:T(8,128)} fusion(bf16[512,1024]{1,0:T(8,128)(2,1)S(1)} %copy-done, f32[256,512]{1,0:T(8,128)S(1)} %get-tuple-element.28, f32[512]{0:T(512)S(1)} %convert_element_type.94, f32[512]{0:T(512)S(1)} %get-tuple-element.8, f32[512]{0:T(512)S(1)} %copy-done.3, s32[512]{0:T(512)S(1)} %bitcast.85, s32[512]{0:T(512)S(1)} %bitcast.88, ...), kind=kOutput, calls=%fused_computation.35 | convolution fusion | flops 275382272 | bytes 2661376 | tf_op jit(solution)/shard_map/dot_general | solution.py:100
  48.5 0.0 reduce-scatter.5.cloned.1.call-update
  48.5 0.0 reduce-scatter.3.cloned.1.call-start
  48.5 2.7 %fusion.16 = f32[512,1024]{1,0:T(8,128)} fusion(bf16[256,1024]{1,0:T(8,128)(2,1)S(1)} %constant_dynamic-update-slice_fusion, f32[256,512]{1,0:T(8,128)S(1)} %get-tuple-element.28, f32[512]{0:T(512)S(1)} %convert_element_type.94, f32[512]{0:T(512)S(1)} %get-tuple-element.8, f32[512]{0:T(512)S(1)} %copy-done.3, s32[512]{0:T(512)S(1)} %bitcast.86, ...), kind=kOutput, calls=%fused_computation.36 | convolution fusion | flops 275382272 | bytes 3185664 | tf_op jit(solution)/shard_map/dot_general | solution.py:93
  51.3 0.0 reduce-scatter.3.cloned.1.call-update
  51.3 58.2 %reduce-scatter.5.cloned.1.call-done = f32[32,1024]{1,0:T(8,128)} async-done(((f32[256,1024]{1,0:T(8,128)}), f32[32,1024]{1,0:T(8,128)}) %reduce-scatter.5.cloned.1.call-update) | async-done | bytes 131088 | tf_op jit(solution)/shard_map/reduce_scatter | solution.py:99
  109.5 11.6 %reduce-scatter.3.cloned.1.call-done = f32[256,1024]{1,0:T(8,128)} async-done(((f32[512,1024]{1,0:T(8,128)}), f32[256,1024]{1,0:T(8,128)}) %reduce-scatter.3.cloned.1.call-update) | async-done | bytes 1048592 | tf_op jit(solution)/shard_map/reduce_scatter | solution.py:98
  (11 shorter events, 0.1 us)
Async XLA Ops:
  7.2 9.5 %copy-start.2 = (s32[512]{0:T(512)S(1)}, s32[512]{0:T(512)}, u32[]{:S(2)}) copy-start(s32[512]{0:T(512)} %param.7) | copy-start | bytes 6148
  7.2 9.5 %copy-start.1 = (s32[512,16]{0,1:T(8,128)S(1)}, s32[512,16]{0,1:T(8,128)}, u32[]{:S(2)}) copy-start(s32[512,16]{0,1:T(8,128)} %param.8) | copy-start | bytes 98308
  7.2 30.5 %all-gather.2.cloned.1.call-start = ((), (), s32[]{:S(2)}) async-start(), calls=%async_computation.2 | async-start | bytes 1572864 | tf_op jit(solution)/shard_map/all_gather | solution.py:26
  8.2 8.5 %collective-permute-start = (bf16[32,1024]{1,0:T(8,128)(2,1)S(1)}, bf16[32,1024]{1,0:T(8,128)(2,1)S(1)}, u32[]{:S(2)}, u32[]{:S(2)}) collective-permute-start(bf16[32,1024]{1,0:T(8,128)(2,1)S(1)} %get-tuple-element.10), channel_id=1, source_target_pairs={{0,2},{2,4},{4,6},{6,8},{8,10},{10,12},{12,14},{14,0},{1,3},{3,5},... | collective-permute-start | bytes 196616 | tf_op jit(solution)/shard_map/ppermute | solution.py:41
  11.2 5.7 %collective-permute-start.1 = (bf16[32,1024]{1,0:T(8,128)(2,1)S(1)}, bf16[32,1024]{1,0:T(8,128)(2,1)S(1)}, u32[]{:S(2)}, u32[]{:S(2)}) collective-permute-start(bf16[32,1024]{1,0:T(8,128)(2,1)S(1)} %get-tuple-element.10), channel_id=1, source_target_pairs={{0,14},{2,0},{4,2},{6,4},{8,6},{10,8},{12,10},{14,12},{1,15},{3,1}... | collective-permute-start | bytes 196616 | tf_op jit(solution)/shard_map/ppermute | solution.py:46
  16.4 29.7 %copy-start.3 = (f32[512]{0:T(512)S(1)}, f32[512]{0:T(512)}, u32[]{:S(2)}) copy-start(f32[512]{0:T(512)} %param.9) | copy-start | bytes 6148
  16.4 93.1 %reduce-scatter.5.cloned.1.call-start = ((), (), s32[]{:S(2)}) async-start(), calls=%async_computation.4 | async-start | bytes 1179648 | tf_op jit(solution)/shard_map/reduce_scatter | solution.py:99
  16.8 7.0 %collective-permute-start.2 = (bf16[32,1024]{1,0:T(8,128)(2,1)S(1)}, bf16[32,1024]{1,0:T(8,128)(2,1)S(1)}, u32[]{:S(2)}, u32[]{:S(2)}) collective-permute-start(bf16[32,1024]{1,0:T(8,128)(2,1)S(1)} %collective-permute-done), channel_id=1, source_target_pairs={{0,2},{2,4},{4,6},{6,8},{8,10},{10,12},{12,14},{14,0},{1,3},{3,5},... | collective-permute-start | bytes 196616 | tf_op jit(solution)/shard_map/ppermute | solution.py:41
  16.9 6.9 %collective-permute-start.3 = (bf16[32,1024]{1,0:T(8,128)(2,1)S(1)}, bf16[32,1024]{1,0:T(8,128)(2,1)S(1)}, u32[]{:S(2)}, u32[]{:S(2)}) collective-permute-start(bf16[32,1024]{1,0:T(8,128)(2,1)S(1)} %collective-permute-done.1), channel_id=1, source_target_pairs={{0,14},{2,0},{4,2},{6,4},{8,6},{10,8},{12,10},{14,12},{1,15},{3,1}... | collective-permute-start | bytes 196616 | tf_op jit(solution)/shard_map/ppermute | solution.py:46
  23.8 7.0 %collective-permute-start.4 = (bf16[32,1024]{1,0:T(8,128)(2,1)S(1)}, bf16[32,1024]{1,0:T(8,128)(2,1)S(1)}, u32[]{:S(2)}, u32[]{:S(2)}) collective-permute-start(bf16[32,1024]{1,0:T(8,128)(2,1)S(1)} %collective-permute-done.2), channel_id=1, source_target_pairs={{0,2},{2,4},{4,6},{6,8},{8,10},{10,12},{12,14},{14,0},{1,3},{3,5},... | collective-permute-start | bytes 196616 | tf_op jit(solution)/shard_map/ppermute | solution.py:41
  23.8 7.0 %collective-permute-start.5 = (bf16[32,1024]{1,0:T(8,128)(2,1)S(1)}, bf16[32,1024]{1,0:T(8,128)(2,1)S(1)}, u32[]{:S(2)}, u32[]{:S(2)}) collective-permute-start(bf16[32,1024]{1,0:T(8,128)(2,1)S(1)} %collective-permute-done.3), channel_id=1, source_target_pairs={{0,14},{2,0},{4,2},{6,4},{8,6},{10,8},{12,10},{14,12},{1,15},{3,1}... | collective-permute-start | bytes 196616 | tf_op jit(solution)/shard_map/ppermute | solution.py:46
  30.7 7.0 %collective-permute-start.6 = (bf16[32,1024]{1,0:T(8,128)(2,1)S(1)}, bf16[32,1024]{1,0:T(8,128)(2,1)S(1)}, u32[]{:S(2)}, u32[]{:S(2)}) collective-permute-start(bf16[32,1024]{1,0:T(8,128)(2,1)S(1)} %collective-permute-done.4), channel_id=1, source_target_pairs={{0,2},{2,4},{4,6},{6,8},{8,10},{10,12},{12,14},{14,0},{1,3},{3,5},... | collective-permute-start | bytes 196616 | tf_op jit(solution)/shard_map/ppermute | solution.py:41
  37.7 8.4 %copy-start = (bf16[512,1024]{1,0:T(8,128)(2,1)S(1)}, bf16[512,1024]{1,0:T(8,128)(2,1)}, u32[]{:S(2)}) copy-start(bf16[512,1024]{1,0:T(8,128)(2,1)} %all-gather.2.cloned.1.call-done) | copy-start | bytes 3145732
  48.5 72.6 %reduce-scatter.3.cloned.1.call-start = ((), (), s32[]{:S(2)}) async-start(), calls=%async_computation.3 | async-start | bytes 3145728 | tf_op jit(solution)/shard_map/reduce_scatter | solution.py:98
Sparse Core Ops, SparseCore 0:
  16.6 7.7 all-gather.1
  48.6 60.8 reduce-scatter.4
  112.4 8.6 reduce-scatter.2
